TPU v7x, 32 devices: a whole 2x2x4 slice. The times are simulated.
32 devices in a mesh: atm: 8 (over y, x, core), xg: 4 (over z).
Axes of the slice: x: 2, y: 2, z: 4, core: 2. Of those that a mesh axis runs over, the one named last changes fastest.
Arguments:
- fields_now: float32 [128, 48, 52, 128], P('atm', None, 'xg'), may hold values from -6 to 6
- upper: float32 [128, 48, 128], P(('atm', 'xg')), may hold values from 0.05 to 20
- lower: float32 [128, 48, 128], P(('atm', 'xg')), may hold values from 0.05 to 20
- surface_gain: float32 [128, 128], P(('atm', 'xg')), may hold values from 0.3 to 3
- route: int32 [8, 32, 2], P('atm'), may hold values from 0 to 16
- margin_slot: int32 [32, 96], P(('atm', 'xg')), may hold values from 0 to 15
- margin_block: int32 [32, 96], P(('atm', 'xg')), may hold values from 0 to 15
- margin_count: int32 [32], P(('atm', 'xg')), may hold values from 12 to 96, as said below
- margin_weight: float32 [32, 96, 128, 128], P(('atm', 'xg')), may hold values from 0 to 0.03
- surface_value: float32 [512, 52, 128], P(('atm', 'xg')), may hold values from -6 to 6
- exchange_coef: float32 [512, 128], P(('atm', 'xg')), may hold values from 0.05 to 2
- land_mask: int32 [512, 128], P(('atm', 'xg')), may hold values 0 or 1
- land_gain: float32 [512, 128], P(('atm', 'xg')), may hold values from 0.2 to 5
Outputs:
- fields_next: float32 [128, 48, 52, 128], P('atm', None, 'xg')
- surface_flux: float32 [512, 52, 128], P(('atm', 'xg'))
Inputs may be any that keep to these rules, and one draw needn't show every extreme that they name: `route`: the value 16 marks an empty slot; other values name a local column block of the sending atmosphere index. `margin_slot`: A value s names slot s % 2 from atmosphere index s // 2. `margin_count`: margins from this count on are padding; some owner has all 96 live.
All inputs are finite; a program needn't handle non-finite values. No bound on the sum of `land_mask` on one device may be relied on, other than what follows from the above.
Results may differ from a plain program's by a relative error of at most 0.0003.
Values sent between devices are 32-bit elements; how exact they have to be, the bound alone decides.
No kernel may reach another device: no remote copies, remote signals or barrier semaphores. Data moves between devices by JAX's collectives and lax.ppermute only.
A program may use at most 128 MiB of HBM per device.

v0:
```python
import functools
import math

import jax
import jax.numpy as jnp
from jax import lax
from jax.experimental import pallas as pl
from jax.experimental.pallas import tpu as pltpu
from jax.sharding import PartitionSpec as P

F32 = jnp.float32
BF16 = jnp.bfloat16
ROWS = 8
PIECES = 5
MOST = 67043328
ROOMY = 50 << 20


def vmem():
    return pl.BlockSpec(memory_space=pltpu.VMEM)


def smem():
    return pl.BlockSpec(memory_space=pltpu.SMEM)


def hbm():
    return pl.BlockSpec(memory_space=pltpu.HBM)


def params(limit):
    return pltpu.CompilerParams(vmem_limit_bytes=limit)


def round_up(value, step):
    return -(-value // step) * step


def split(value):
    high = value.astype(BF16).astype(F32)
    return jnp.concatenate([high, value - high], 0).astype(BF16)


def factor_kernel(levels, own, upper_hbm, lower_hbm, gain_hbm, first_ref, second_ref,
                  upper_ref, lower_ref, gain_ref, sem):
    copies = [
        pltpu.make_async_copy(source, target, sem.at[i])
        for i, (source, target) in enumerate(
            ((upper_hbm, upper_ref), (lower_hbm, lower_ref), (gain_hbm, gain_ref))
        )
    ]
    for copy in copies:
        copy.start()
    for copy in copies:
        copy.wait()
    carried = jnp.zeros(gain_ref.shape, F32)
    inverse = carried
    for k in range(levels):
        from_above = upper_ref[pl.ds(k, own, stride=levels), :] if k > 0 else jnp.zeros_like(carried)
        from_below = lower_ref[pl.ds(k, own, stride=levels), :] if k < levels - 1 else jnp.zeros_like(carried)
        if k > 0:
            first_ref[k] = from_above * inverse
        inverse = 1.0 / (1.0 + from_above + from_below - from_above * carried)
        carried = from_below * inverse
        second_ref[k] = carried
    first_ref[0] = inverse
    first_ref[levels] = gain_ref[...] * inverse


def factors(upper, lower, surface_gain):
    own, levels, width = upper.shape
    return pl.pallas_call(
        functools.partial(factor_kernel, levels, own),
        out_shape=(
            jax.ShapeDtypeStruct((levels + 1, own, width), F32),
            jax.ShapeDtypeStruct((levels, own, width), F32),
        ),
        in_specs=[hbm()] * 3,
        out_specs=(vmem(), vmem()),
        scratch_shapes=[
            pltpu.VMEM((own * levels, width), F32),
            pltpu.VMEM((own * levels, width), F32),
            pltpu.VMEM((own, width), F32),
            pltpu.SemaphoreType.DMA((3,)),
        ],
        compiler_params=params(MOST),
        cost_estimate=pl.CostEstimate(flops=1000000, bytes_accessed=400000, transcendentals=30000),
        name="factors",
    )(upper.reshape(own * levels, width), lower.reshape(own * levels, width), surface_gain)


def bundles(shares):
    pieces = min(PIECES, shares)
    edges = [i * shares // pieces for i in range(pieces + 1)]
    return list(zip(edges[:-1], edges[1:]))


def field_copies(me, groups, own, fields_ref, held_ref, sem, piece, out):
    low, high = bundles(held_ref.shape[0])[piece]
    copies = []
    for q in range(groups):
        base = lax.rem(me - q + groups, groups) * own
        for i in range(own):
            far = fields_ref.at[base + i, pl.ds(low, high - low)]
            near = held_ref.at[pl.ds(low, high - low), :, q * own + i, :]
            pair = (near, far) if out else (far, near)
            copies.append(pltpu.make_async_copy(*pair, sem.at[piece]))
    return copies


def fetch_fields(me, groups, own, fields_ref, held_ref, sem):
    for piece in range(len(bundles(held_ref.shape[0]))):
        for copy in field_copies(me, groups, own, fields_ref, held_ref, sem, piece, False):
            copy.start()


def wait_piece(held_ref, sem, piece):
    low, high = bundles(held_ref.shape[0])[piece]
    part = held_ref.at[pl.ds(low, high - low)]
    pltpu.make_async_copy(part, part, sem.at[piece]).wait()


def bottom_kernel(groups, own, rows, slots, me_ref, place_ref, *refs):
    parts, fields_ref, send_ref, held_ref, weight_ref, value_ref, own_ref, sem, own_sem = (
        refs[:groups], *refs[groups:]
    )
    fetch = pltpu.make_async_copy(parts[0], own_ref, own_sem)
    fetch.start()
    fetch_fields(me_ref[0], groups, own, fields_ref, held_ref, sem)
    blocks = groups * own
    pitch = round_up(rows, ROWS)
    levels = held_ref.shape[1]
    shares = held_ref.shape[0]
    for q in range(1, groups):
        weight_ref[:, q * own:(q + 1) * own, :] = parts[q][...]
    fetch.wait()
    weight_ref[:, :own, :] = own_ref[...]
    weight = weight_ref[0]
    for k in range(levels - 1, -1, -1):
        ratio = weight_ref[k]
        weight_ref[k] = weight
        weight = weight * ratio
    value_ref[...] = jnp.zeros_like(value_ref)
    value_ref[pl.ds(shares, blocks, stride=pitch), :] = weight_ref[levels]
    for piece, (low, high) in enumerate(bundles(shares)):
        wait_piece(held_ref, sem, piece)
        sums = {}
        for k in range(levels):
            weight = weight_ref[k]
            for f in range(low, high):
                term = weight * held_ref[f, k]
                slot = (f, k % 2)
                sums[slot] = sums[slot] + term if slot in sums else term
        for f in range(low, high):
            value_ref[pl.ds(f, blocks, stride=pitch), :] = sums[f, 0] + sums[f, 1]
    for d in range(send_ref.shape[0] // (rows * slots)):
        for p in range(slots):
            start = pl.multiple_of(place_ref[d * slots + p] * pitch, pitch)
            send_ref[pl.ds(d * rows * slots + p, rows, stride=slots), :] = value_ref[pl.ds(start, rows), :]


def bottoms(me, place, parts, fields, owners, slots, rows):
    blocks, shares, levels, width = fields.shape
    groups = len(parts)
    own = blocks // groups
    return pl.pallas_call(
        functools.partial(bottom_kernel, groups, own, rows, slots),
        out_shape=jax.ShapeDtypeStruct((owners * rows * slots, width), F32),
        in_specs=[smem(), smem(), hbm()] + [vmem()] * (groups - 1) + [hbm()],
        out_specs=vmem(),
        scratch_shapes=[
            pltpu.VMEM((shares, levels, blocks, width), F32),
            pltpu.VMEM((levels + 1, blocks, width), F32),
            pltpu.VMEM(((blocks + 1) * round_up(rows, ROWS), width), F32),
            pltpu.VMEM((levels + 1, own, width), F32),
            pltpu.SemaphoreType.DMA((len(bundles(shares)),)),
            pltpu.SemaphoreType.DMA(()),
        ],
        compiler_params=params(ROOMY),
        cost_estimate=pl.CostEstimate(flops=4000000, bytes_accessed=7000000, transcendentals=0),
        name="bottoms",
    )(me, place, *parts, fields)


def split_kernel(weight_ref, out_ref):
    value = weight_ref[...]
    size = weight_ref.shape[1]
    high = value.astype(BF16)
    out_ref[:, :size, :] = high
    out_ref[:, size:, :] = (value - high.astype(F32)).astype(BF16)


def split_weights(weight, start, stop, step=8):
    _, cells, columns = weight.shape
    count = stop - start
    step = math.gcd(step, math.gcd(start, count))
    first = start // step
    return pl.pallas_call(
        split_kernel,
        grid=(count // step,),
        out_shape=jax.ShapeDtypeStruct((count, 2 * cells, columns), BF16),
        in_specs=[pl.BlockSpec((step, cells, columns), lambda i: (first + i, 0, 0))],
        out_specs=pl.BlockSpec((step, 2 * cells, columns), lambda i: (i, 0, 0)),
        compiler_params=params(ROOMY),
        cost_estimate=pl.CostEstimate(flops=2500000, bytes_accessed=6500000, transcendentals=0),
        name="split_weights",
    )(weight)


def margin_kernel(
    groups, rows, slots, gain_row, unroll,
    slot_ref, block_ref, count_ref, weight_a, weight_b, got_ref, surface_ref, coef_ref, mask_ref, land_ref,
    reply_ref, flux_ref,
    weight_ref, value_ref, cell_ref, two_ref, back_ref, stack_ref, sem,
):
    margins = weight_ref.shape[0]
    chunks = sem.shape[0]
    size = margins // chunks
    half = weight_a.shape[0] // size

    def fetch(c):
        source = weight_a if c < half else weight_b
        return pltpu.make_async_copy(
            source.at[pl.ds((c if c < half else c - half) * size, size)], weight_ref.at[pl.ds(c * size, size)], sem.at[c]
        )

    for c in range(chunks):
        fetch(c).start()
    tall = groups * rows
    top = round_up(tall, 2 * ROWS)
    columns = weight_ref.shape[2]
    sources = value_ref.shape[0] // slots
    cells = surface_ref.shape[0]
    count = count_ref[0]
    for a in range(sources):
        for p in range(slots):
            for g in range(groups):
                stack_ref[a * slots + p, g * rows:(g + 1) * rows, :] = (
                    got_ref[pl.ds((a * groups + g) * rows * slots + p, rows, stride=slots), :]
                )
    for s in range(sources * slots):
        value_ref[s] = split(stack_ref[s])
    cell_ref[...] = jnp.zeros_like(cell_ref)
    back_ref[...] = jnp.zeros_like(back_ref)

    for c in range(chunks):
        fetch(c).wait()

        @pl.loop(0, size // unroll)
        def _(step):
            for u in range(unroll):
                k = c * size + step * unroll + u
                target = jnp.where(k < count, block_ref[k], cells)
                one = lax.dot_general(
                    value_ref[slot_ref[k]], weight_ref[k, :columns], (((1,), (1,)), ((), ())),
                    preferred_element_type=F32,
                )
                two = lax.dot_general(
                    value_ref[slot_ref[k], :top], weight_ref[k, columns:], (((1,), (1,)), ((), ())),
                    preferred_element_type=F32,
                )
                cell_ref[target] += one[:tall] + (one[tall:] + two[:tall])

    for j in range(cells):
        cell = cell_ref[j]
        coef = coef_ref[j:j + 1, :]
        land = mask_ref[j:j + 1, :].astype(F32) * land_ref[j:j + 1, :]
        scale = coef / (1.0 + coef * (cell[gain_row:gain_row + 1, :] + land))
        flux = scale * (surface_ref[j] - cell)
        flux_ref[j] = flux
        two_ref[j] = split(flux)

    @pl.loop(0, margins // unroll)
    def _(step):
        for u in range(unroll):
            k = step * unroll + u
            target = jnp.where(k < count, slot_ref[k], sources * slots)
            one = jnp.dot(two_ref[block_ref[k]], weight_ref[k, :columns], preferred_element_type=F32)
            two = jnp.dot(
                two_ref[block_ref[k], :top], weight_ref[k, columns:], preferred_element_type=F32
            )
            back_ref[target] += one[:tall] + (one[tall:] + two[:tall])

    for a in range(sources):
        for p in range(slots):
            for g in range(groups):
                reply_ref[pl.ds((a * groups + g) * rows * slots + p, rows, stride=slots), :] = (
                    back_ref[a * slots + p, g * rows:(g + 1) * rows, :]
                )


def margins_stage(slot, block, count, weights_a, weights_b, got, surface, coef, mask, land,
                  groups, rows, slots, gain_row):
    part, twice, columns = weights_a.shape
    margins = part + weights_b.shape[0]
    width = got.shape[1]
    owners = got.shape[0] // (rows * slots)
    cells, tall, _ = surface.shape
    sources = owners // groups
    chunks = 6
    unroll = math.gcd(16, margins // chunks)
    return pl.pallas_call(
        functools.partial(margin_kernel, groups, rows, slots, gain_row, unroll),
        out_shape=(
            jax.ShapeDtypeStruct(got.shape, F32),
            jax.ShapeDtypeStruct(surface.shape, F32),
        ),
        in_specs=[smem()] * 3 + [hbm()] * 2 + [vmem()] * 5,
        out_specs=(vmem(), vmem()),
        scratch_shapes=[
            pltpu.VMEM((margins, twice, columns), BF16),
            pltpu.VMEM((sources * slots, 2 * tall, width), BF16),
            pltpu.VMEM((cells + 1, tall, width), F32),
            pltpu.VMEM((cells, 2 * tall, width), BF16),
            pltpu.VMEM((sources * slots + 1, tall, width), F32),
            pltpu.VMEM((sources * slots, tall, width), F32),
            pltpu.SemaphoreType.DMA((chunks,)),
        ],
        compiler_params=params(ROOMY),
        cost_estimate=pl.CostEstimate(flops=800000000, bytes_accessed=8000000, transcendentals=0),
        name="margins",
    )(slot, block, count, weights_a, weights_b, got, surface, coef, mask, land)


def unfold(groups, own, firsts, seconds, factor_ref, gain_ref):
    levels = factor_ref.shape[0] // 3
    for q in range(groups):
        factor_ref[:levels, q * own:(q + 1) * own, :] = firsts[q][:levels]
        factor_ref[2 * levels:, q * own:(q + 1) * own, :] = seconds[q][...]
        gain_ref[q * own:(q + 1) * own, :] = firsts[q][levels]
    above = factor_ref[2 * levels]
    inverse = 1.0 - above
    factor_ref[levels] = inverse
    for k in range(1, levels):
        carry = factor_ref[2 * levels + k]
        inverse = (1.0 - carry) * inverse / (inverse + factor_ref[k] * (1.0 - above))
        factor_ref[levels + k] = inverse
        above = carry


def finish_kernel(groups, own, rows, slots, me_ref, place_ref, answer_ref, *refs):
    firsts, seconds, fields_ref, out_ref, held_ref, factor_ref, gain_ref, flux_ref, sem, out_sem = (
        refs[:groups], refs[groups:2 * groups], *refs[2 * groups:]
    )
    me = me_ref[0]
    fetch_fields(me, groups, own, fields_ref, held_ref, sem)
    unfold(groups, own, firsts, seconds, factor_ref, gain_ref)
    shares, levels, blocks, _ = held_ref.shape
    flux_ref[...] = jnp.zeros_like(flux_ref)
    pitch = round_up(rows, ROWS)
    for d in range(answer_ref.shape[0] // (rows * slots)):
        for p in range(slots):
            start = pl.multiple_of(place_ref[d * slots + p] * pitch, pitch)
            flux_ref[pl.ds(start, rows), :] += (
                answer_ref[pl.ds(d * rows * slots + p, rows, stride=slots), :]
            )
    for piece, (low, high) in enumerate(bundles(shares)):
        wait_piece(held_ref, sem, piece)
        span = range(low, high)
        state = {f: held_ref[f, 0] for f in span}
        for k in range(1, levels):
            ratio = factor_ref[k]
            for f in span:
                state[f] = held_ref[f, k] + ratio * state[f]
                if k < levels - 1:
                    held_ref[f, k] = state[f]
        inverse = factor_ref[2 * levels - 1]
        for f in span:
            flux = flux_ref[pl.ds(f, blocks, stride=pitch), :]
            state[f] = inverse * state[f] + gain_ref[...] * flux
            held_ref[f, levels - 1] = state[f]
        for k in range(levels - 2, -1, -1):
            inverse, carry = factor_ref[levels + k], factor_ref[2 * levels + k]
            for f in span:
                state[f] = inverse * held_ref[f, k] + carry * state[f]
                held_ref[f, k] = state[f]
        for copy in field_copies(me, groups, own, out_ref, held_ref, out_sem, piece, True):
            copy.start()
    for piece in range(len(bundles(shares))):
        wait_piece(held_ref, out_sem, piece)


def finish(me, place, answer, firsts, seconds, fields, rows, slots):
    blocks, shares, levels, width = fields.shape
    groups = len(firsts)
    return pl.pallas_call(
        functools.partial(finish_kernel, groups, blocks // groups, rows, slots),
        out_shape=jax.ShapeDtypeStruct((blocks, shares, levels, width), F32),
        in_specs=[smem(), smem(), vmem()] + [vmem()] * (2 * groups) + [hbm()],
        out_specs=hbm(),
        scratch_shapes=[
            pltpu.VMEM((shares, levels, blocks, width), F32),
            pltpu.VMEM((3 * levels, blocks, width), F32),
            pltpu.VMEM((blocks, width), F32),
            pltpu.VMEM(((blocks + 1) * round_up(rows, ROWS), width), F32),
            pltpu.SemaphoreType.DMA((len(bundles(shares)),)),
            pltpu.SemaphoreType.DMA((len(bundles(shares)),)),
        ],
        compiler_params=params(ROOMY),
        cost_estimate=pl.CostEstimate(flops=8000000, bytes_accessed=12000000, transcendentals=0),
        name="finish",
    )(me, place, answer, *firsts, *seconds, fields)


def per_device(
    fields_now, upper, lower, surface_gain, route, margin_slot, margin_block, margin_count,
    margin_weight, surface_value, exchange_coef, land_mask, land_gain,
):
    groups = lax.axis_size("xg")
    me = lax.axis_index("xg").astype(jnp.int32)
    blocks, _, shares, width = fields_now.shape
    own = blocks // groups
    rows = shares + 1
    owners, slots = route.shape[1:]
    cells = surface_value.shape[0]

    def shift(array, by):
        return lax.ppermute(array, "xg", [(i, (i + by) % groups) for i in range(groups)])

    def shared(array):
        return [array] + [shift(array, by) for by in range(1, groups)]

    def exchange(array):
        array = array.reshape(owners, rows, slots, width)
        array = lax.all_to_all(array, ("atm", "xg"), split_axis=0, concat_axis=0, tiled=True)
        return array.reshape(owners * rows * slots, width)

    fields = fields_now.transpose(0, 2, 1, 3)
    first, second = factors(upper, lower, surface_gain)
    firsts = shared(first)
    routing = route[0].reshape(owners * slots)
    place = jnp.where(
        routing < blocks,
        lax.rem(me - routing // own + groups, groups) * own + routing % own,
        blocks,
    ).astype(jnp.int32)
    me = me[None]
    weights_a = split_weights(margin_weight[0], 0, margin_weight.shape[1] // 6)
    weights_b = split_weights(margin_weight[0], margin_weight.shape[1] // 6, margin_weight.shape[1])
    surface = jnp.pad(
        surface_value.reshape(cells, groups, shares, width),
        ((0, 0), (0, 0), (0, rows - shares), (0, 0)),
    ).reshape(cells, groups * rows, width)
    send = bottoms(me, place, firsts, fields, owners, slots, rows)
    got = exchange(send)
    seconds = [second] + [None] * (groups - 1)
    seconds[1], seconds[groups - 1] = shift(second, 1), shift(second, groups - 1)
    for by in range(groups - 2, 1, -1):
        seconds[by] = shift(seconds[by + 1], groups - 1)
    reply, flux = margins_stage(
        margin_slot[0], margin_block[0], margin_count, weights_a, weights_b, got, surface,
        exchange_coef, land_mask, land_gain, groups, rows, slots, shares,
    )
    answer = exchange(reply)
    surface_flux = flux.reshape(cells, groups, rows, width)[:, :, :shares].reshape(
        cells, groups * shares, width
    )
    out = finish(me, place, answer, firsts, seconds, fields, rows, slots)
    return out.transpose(0, 2, 1, 3), surface_flux


def solution(mesh):
    in_specs = (
        P("atm", None, "xg", None),
        P(("atm", "xg"), None, None),
        P(("atm", "xg"), None, None),
        P(("atm", "xg"), None),
        P("atm", None, None),
        P(("atm", "xg"), None),
        P(("atm", "xg"), None),
        P(("atm", "xg")),
        P(("atm", "xg"), None, None, None),
        P(("atm", "xg"), None, None),
        P(("atm", "xg"), None),
        P(("atm", "xg"), None),
        P(("atm", "xg"), None),
    )
    out_specs = (P("atm", None, "xg", None), P(("atm", "xg"), None, None))
    return jax.shard_map(
        per_device, mesh=mesh, in_specs=in_specs, out_specs=out_specs, check_vma=False
    )
```

profile of v0, /device:TPU:0, one launch (start us, length us, event | category | flops | bytes accessed | tf_op | source)
XLA Modules:
  0.0 78.8 jit_solution(2742040166513013354)
XLA Ops:
  0.6 2.1 %factors.1 = (f32[49,4,128]{2,1,0:T(4,128)}, f32[48,4,128]{2,1,0:T(4,128)}) custom-call(f32[192,128]{1,0:T(8,128)} %bitcast.29, f32[192,128]{1,0:T(8,128)} %bitcast.30, f32[4,128]{1,0:T(4,128)} %gain_hbm.1), custom_call_target="tpu_custom_call" | custom-call | flops 1000000 | bytes 400000 | tf_op jit(solution)/shard_map/factors/pallas_call | solution.py:72
  2.7 3.1 %collective-permute-start = (f32[49,4,128]{2,1,0:T(4,128)}, f32[49,4,128]{2,1,0:T(4,128)S(1)}, u32[]{:S(2)}, u32[]{:S(2)}) collective-permute-start(f32[49,4,128]{2,1,0:T(4,128)} %get-tuple-element.6.refs_0_), channel_id=1, source_target_pairs={{0,1},{1,2},{2,3},{3,0},{4,5},{5,6},{6,7},{7,4},{8,9},{9,10},{10,1... | collective-permute-start | bytes 301064 | tf_op jit(solution)/shard_map/ppermute | solution.py:418
  5.8 2.6 %collective-permute-start.1 = (f32[49,4,128]{2,1,0:T(4,128)}, f32[49,4,128]{2,1,0:T(4,128)S(1)}, u32[]{:S(2)}, u32[]{:S(2)}) collective-permute-start(f32[49,4,128]{2,1,0:T(4,128)} %get-tuple-element.6.refs_0_), channel_id=1, source_target_pairs={{0,2},{1,3},{2,0},{3,1},{4,6},{5,7},{6,4},{7,5},{8,10},{9,11},{10,... | collective-permute-start | bytes 301064 | tf_op jit(solution)/shard_map/ppermute | solution.py:418
  8.4 1.3 %collective-permute-start.2 = (f32[49,4,128]{2,1,0:T(4,128)}, f32[49,4,128]{2,1,0:T(4,128)S(1)}, u32[]{:S(2)}, u32[]{:S(2)}) collective-permute-start(f32[49,4,128]{2,1,0:T(4,128)} %get-tuple-element.6.refs_0_), channel_id=1, source_target_pairs={{0,3},{1,0},{2,1},{3,2},{4,7},{5,4},{6,5},{7,6},{8,11},{9,8},{10,9... | collective-permute-start | bytes 301064 | tf_op jit(solution)/shard_map/ppermute | solution.py:418
  9.8 0.8 copy.18
  10.5 0.1 reshape_squeeze.3
  10.6 1.1 %collective-permute-done.refs_1_ = f32[49,4,128]{2,1,0:T(4,128)S(1)} collective-permute-done((f32[49,4,128]{2,1,0:T(4,128)}, f32[49,4,128]{2,1,0:T(4,128)S(1)}, u32[]{:S(2)}, u32[]{:S(2)}) %collective-permute-start) | collective-permute-done | bytes 100384 | tf_op jit(solution)/shard_map/ppermute | solution.py:418
  11.8 3.5 %collective-permute-done.1.refs_2_ = f32[49,4,128]{2,1,0:T(4,128)S(1)} collective-permute-done((f32[49,4,128]{2,1,0:T(4,128)}, f32[49,4,128]{2,1,0:T(4,128)S(1)}, u32[]{:S(2)}, u32[]{:S(2)}) %collective-permute-start.1) | collective-permute-done | bytes 100384 | tf_op jit(solution)/shard_map/ppermute | solution.py:418
  15.3 0.0 collective-permute-done.2.refs_3_
  15.3 0.0 copy-start
  15.3 0.9 %copy-done = f32[49,4,128]{2,1,0:T(4,128)S(1)} copy-done((f32[49,4,128]{2,1,0:T(4,128)S(1)}, f32[49,4,128]{2,1,0:T(4,128)}, u32[]{:S(2)}) %copy-start) | copy-done | bytes 100376
  16.2 0.0 copy-start.8
  16.2 4.2 %bottoms.1 = f32[896,128]{1,0:T(8,128)} custom-call(s32[1]{0:T(128)} %bitcast.me_ref, s32[64]{0:T(128)S(1)} %compare_select_fusion.2.place_ref, f32[49,4,128]{2,1,0:T(4,128)S(1)} %copy-done, f32[49,4,128]{2,1,0:T(4,128)S(1)} %collective-permute-done.refs_1_, f32[49,4,128]{2,1,0:T(4,128)S(1)} %collective-permute-done.1.refs_2_, ...), custom_call_target="tpu_custom_call" | custom-call | flops 4000000 | bytes 7000000 | tf_op jit(solution)/shard_map/bottoms/pallas_call | solution.py:166
  20.4 5.9 %all-to-all-start = ((f32[32,14,2,128]{3,2,1,0:T(2,128)}), f32[32,14,2,128]{3,2,1,0:T(2,128)S(1)}, u32[]{:S(2)}, u32[]{:S(2)}) async-start(f32[32,14,2,128]{3,2,1,0:T(2,128)} %bitcast.7), calls=%async_computation | async-start | bytes 917504 | tf_op jit(solution)/shard_map/all_to_all | solution.py:425
  26.3 0.0 copy-done.8
  26.4 0.2 copy.19.surface_ref
  27.2 8.1 %split_weights.3.weight_b = bf16[80,256,128]{2,1,0:T(8,128)(2,1)} custom-call(f32[96,128,128]{2,1,0:T(8,128)} %bitcast.20), custom_call_target="tpu_custom_call" | custom-call | flops 2500000 | bytes 6500000 | tf_op jit(solution)/shard_map/split_weights/pallas_call | solution.py:198
  35.3 0.0 copy-start.3
  35.3 0.0 copy-start.4
  35.3 0.0 copy-start.5
  35.3 0.0 copy-start.6
  35.3 0.0 copy-start.7
  35.3 1.3 %split_weights.2.weight_a = bf16[16,256,128]{2,1,0:T(8,128)(2,1)S(1)} custom-call(f32[96,128,128]{2,1,0:T(8,128)} %bitcast.21), custom_call_target="tpu_custom_call" | custom-call | flops 2500000 | bytes 6500000 | tf_op jit(solution)/shard_map/split_weights/pallas_call | solution.py:198
  36.7 0.0 copy-start.2
  36.7 0.0 copy-start.1
  36.7 2.6 %all-to-all-done = f32[32,14,2,128]{3,2,1,0:T(2,128)S(1)} async-done(((f32[32,14,2,128]{3,2,1,0:T(2,128)}), f32[32,14,2,128]{3,2,1,0:T(2,128)S(1)}, u32[]{:S(2)}, u32[]{:S(2)}) %all-to-all-start) | async-done | bytes 458784 | tf_op jit(solution)/shard_map/all_to_all | solution.py:425
  39.3 0.0 copy-done.3
  39.3 0.0 copy-done.4
  39.3 0.0 copy-done.5
  39.3 0.0 copy-done.6
  39.3 0.0 copy-done.7
  39.3 9.6 %margins.1 = (f32[896,128]{1,0:T(8,128)}, f32[16,56,128]{2,1,0:T(8,128)S(1)}) custom-call(s32[96]{0:T(128)S(1)} %bitcast.18, s32[96]{0:T(128)S(1)} %bitcast.19, s32[1]{0:T(128)S(6)} %copy.21.count_ref, bf16[16,256,128]{2,1,0:T(8,128)(2,1)S(1)} %split_weights.2.weight_a, bf16[80,256,128]{2,1,0:T(8,128)(2,1)} %split_weights.3.weight_b, ...), custom_call_target="tpu_custom_call" | custom-call | flops 800000000 | bytes 8000000 | tf_op jit(solution)/shard_map/margins/pallas_call | solution.py:302
  48.9 4.0 %all-to-all-start.1 = ((f32[32,14,2,128]{3,2,1,0:T(2,128)}), f32[32,14,2,128]{3,2,1,0:T(2,128)S(1)}, u32[]{:S(2)}, u32[]{:S(2)}) async-start(f32[32,14,2,128]{3,2,1,0:T(2,128)} %bitcast.11), calls=%async_computation.1 | async-start | bytes 917504 | tf_op jit(solution)/shard_map/all_to_all | solution.py:425
  53.0 0.0 copy-done.2
  53.0 3.7 %collective-permute-start.4 = (f32[48,4,128]{2,1,0:T(4,128)S(1)}, f32[48,4,128]{2,1,0:T(4,128)S(1)}, u32[]{:S(2)}, u32[]{:S(2)}) collective-permute-start(f32[48,4,128]{2,1,0:T(4,128)S(1)} %copy-done.2), channel_id=1, source_target_pairs={{0,3},{1,0},{2,1},{3,2},{4,7},{5,4},{6,5},{7,6},{8,11},{9,8},{10,9... | collective-permute-start | bytes 294920 | tf_op jit(solution)/shard_map/ppermute | solution.py:418
  56.7 0.0 collective-permute-start.3
  56.7 7.3 %collective-permute-done.4.refs_7_ = f32[48,4,128]{2,1,0:T(4,128)S(1)} collective-permute-done((f32[48,4,128]{2,1,0:T(4,128)S(1)}, f32[48,4,128]{2,1,0:T(4,128)S(1)}, u32[]{:S(2)}, u32[]{:S(2)}) %collective-permute-start.4) | collective-permute-done | bytes 98336 | tf_op jit(solution)/shard_map/ppermute | solution.py:418
  64.0 3.8 %collective-permute-start.5 = (f32[48,4,128]{2,1,0:T(4,128)S(1)}, f32[48,4,128]{2,1,0:T(4,128)S(1)}, u32[]{:S(2)}, u32[]{:S(2)}) collective-permute-start(f32[48,4,128]{2,1,0:T(4,128)S(1)} %collective-permute-done.4.refs_7_), channel_id=1, source_target_pairs={{0,3},{1,0},{2,1},{3,2},{4,7},{5,4},{6,5},{7,6},{8,11},{9,8},{10,9... | collective-permute-start | bytes 294920 | tf_op jit(solution)/shard_map/ppermute | solution.py:418
  67.8 0.1 copy.20
  67.9 0.8 %slice.4 = f32[16,4,13,128]{3,0,2,1:T(8,128)} slice(f32[16,4,14,128]{3,0,2,1:T(8,128)S(1)} %bitcast.26), slice={[0:16], [0:4], [0:13], [0:128]} | slice | bytes 851968 | tf_op jit(solution)/shard_map/slice | solution.py:455
  68.7 0.7 collective-permute-done.3.refs_5_
  69.4 4.6 %collective-permute-done.5.refs_6_ = f32[48,4,128]{2,1,0:T(4,128)S(1)} collective-permute-done((f32[48,4,128]{2,1,0:T(4,128)S(1)}, f32[48,4,128]{2,1,0:T(4,128)S(1)}, u32[]{:S(2)}, u32[]{:S(2)}) %collective-permute-start.5) | collective-permute-done | bytes 98336 | tf_op jit(solution)/shard_map/ppermute | solution.py:418
  73.9 0.0 all-to-all-done.1
  73.9 0.0 copy-done.1
  73.9 4.9 %finish.1 = f32[16,13,48,128]{3,2,1,0:T(8,128)} custom-call(s32[1]{0:T(128)} %bitcast.me_ref, s32[64]{0:T(128)S(1)} %compare_select_fusion.2.place_ref, f32[896,128]{1,0:T(8,128)S(1)} %bitcast.17, f32[49,4,128]{2,1,0:T(4,128)S(1)} %copy-done.1, f32[49,4,128]{2,1,0:T(4,128)S(1)} %collective-permute-done.refs_1_, ...), custom_call_target="tpu_custom_call" | custom-call | flops 8000000 | bytes 12000000 | tf_op jit(solution)/shard_map/finish/pallas_call | solution.py:386
  (2 shorter events, 0.1 us)
Async XLA Ops:
  2.7 9.1 %collective-permute-start = (f32[49,4,128]{2,1,0:T(4,128)}, f32[49,4,128]{2,1,0:T(4,128)S(1)}, u32[]{:S(2)}, u32[]{:S(2)}) collective-permute-start(f32[49,4,128]{2,1,0:T(4,128)} %get-tuple-element.6.refs_0_), channel_id=1, source_target_pairs={{0,1},{1,2},{2,3},{3,0},{4,5},{5,6},{6,7},{7,4},{8,9},{9,10},{10,1... | collective-permute-start | bytes 301064 | tf_op jit(solution)/shard_map/ppermute | solution.py:418
  5.8 9.5 %collective-permute-start.1 = (f32[49,4,128]{2,1,0:T(4,128)}, f32[49,4,128]{2,1,0:T(4,128)S(1)}, u32[]{:S(2)}, u32[]{:S(2)}) collective-permute-start(f32[49,4,128]{2,1,0:T(4,128)} %get-tuple-element.6.refs_0_), channel_id=1, source_target_pairs={{0,2},{1,3},{2,0},{3,1},{4,6},{5,7},{6,4},{7,5},{8,10},{9,11},{10,... | collective-permute-start | bytes 301064 | tf_op jit(solution)/shard_map/ppermute | solution.py:418
  8.4 6.9 %collective-permute-start.2 = (f32[49,4,128]{2,1,0:T(4,128)}, f32[49,4,128]{2,1,0:T(4,128)S(1)}, u32[]{:S(2)}, u32[]{:S(2)}) collective-permute-start(f32[49,4,128]{2,1,0:T(4,128)} %get-tuple-element.6.refs_0_), channel_id=1, source_target_pairs={{0,3},{1,0},{2,1},{3,2},{4,7},{5,4},{6,5},{7,6},{8,11},{9,8},{10,9... | collective-permute-start | bytes 301064 | tf_op jit(solution)/shard_map/ppermute | solution.py:418
  15.3 0.9 %copy-start = (f32[49,4,128]{2,1,0:T(4,128)S(1)}, f32[49,4,128]{2,1,0:T(4,128)}, u32[]{:S(2)}) copy-start(f32[49,4,128]{2,1,0:T(4,128)} %get-tuple-element.6.refs_0_) | copy-start | bytes 301060
  16.2 10.1 %copy-start.8 = (f32[16,52,128]{2,0,1:T(8,128)S(1)}, f32[16,52,128]{2,0,1:T(8,128)}, u32[]{:S(2)}) copy-start(f32[16,52,128]{2,0,1:T(8,128)} %param.22) | copy-start | bytes 1277956
  20.4 18.9 %all-to-all-start = ((f32[32,14,2,128]{3,2,1,0:T(2,128)}), f32[32,14,2,128]{3,2,1,0:T(2,128)S(1)}, u32[]{:S(2)}, u32[]{:S(2)}) async-start(f32[32,14,2,128]{3,2,1,0:T(2,128)} %bitcast.7), calls=%async_computation | async-start | bytes 917504 | tf_op jit(solution)/shard_map/all_to_all | solution.py:425
  35.3 4.0 %copy-start.3 = (f32[16,128]{1,0:T(8,128)S(1)}, f32[16,128]{1,0:T(8,128)}, u32[]{:S(2)}) copy-start(f32[16,128]{1,0:T(8,128)} %coef_ref.1) | copy-start | bytes 24580
  35.3 4.0 %copy-start.4 = (s32[16,128]{1,0:T(8,128)S(1)}, s32[16,128]{1,0:T(8,128)}, u32[]{:S(2)}) copy-start(s32[16,128]{1,0:T(8,128)} %mask_ref.1) | copy-start | bytes 24580
  35.3 4.0 %copy-start.5 = (f32[16,128]{1,0:T(8,128)S(1)}, f32[16,128]{1,0:T(8,128)}, u32[]{:S(2)}) copy-start(f32[16,128]{1,0:T(8,128)} %land_ref.1) | copy-start | bytes 24580
  35.3 4.0 %copy-start.6 = (s32[1,96]{1,0:T(1,128)S(1)}, s32[1,96]{1,0:T(1,128)}, u32[]{:S(2)}) copy-start(s32[1,96]{1,0:T(1,128)} %param.18) | copy-start | bytes 1156
  35.3 4.0 %copy-start.7 = (s32[1,96]{1,0:T(1,128)S(1)}, s32[1,96]{1,0:T(1,128)}, u32[]{:S(2)}) copy-start(s32[1,96]{1,0:T(1,128)} %param.19) | copy-start | bytes 1156
  36.7 16.3 %copy-start.2 = (f32[48,4,128]{2,1,0:T(4,128)S(1)}, f32[48,4,128]{2,1,0:T(4,128)}, u32[]{:S(2)}) copy-start(f32[48,4,128]{2,1,0:T(4,128)} %get-tuple-element.8.refs_4_) | copy-start | bytes 294916
  36.7 37.2 %copy-start.1 = (f32[49,4,128]{2,1,0:T(4,128)S(1)}, f32[49,4,128]{2,1,0:T(4,128)}, u32[]{:S(2)}) copy-start(f32[49,4,128]{2,1,0:T(4,128)} %get-tuple-element.6.refs_0_) | copy-start | bytes 301060
  48.9 25.0 %all-to-all-start.1 = ((f32[32,14,2,128]{3,2,1,0:T(2,128)}), f32[32,14,2,128]{3,2,1,0:T(2,128)S(1)}, u32[]{:S(2)}, u32[]{:S(2)}) async-start(f32[32,14,2,128]{3,2,1,0:T(2,128)} %bitcast.11), calls=%async_computation.1 | async-start | bytes 917504 | tf_op jit(solution)/shard_map/all_to_all | solution.py:425
  53.0 11.0 %collective-permute-start.4 = (f32[48,4,128]{2,1,0:T(4,128)S(1)}, f32[48,4,128]{2,1,0:T(4,128)S(1)}, u32[]{:S(2)}, u32[]{:S(2)}) collective-permute-start(f32[48,4,128]{2,1,0:T(4,128)S(1)} %copy-done.2), channel_id=1, source_target_pairs={{0,3},{1,0},{2,1},{3,2},{4,7},{5,4},{6,5},{7,6},{8,11},{9,8},{10,9... | collective-permute-start | bytes 294920 | tf_op jit(solution)/shard_map/ppermute | solution.py:418
  56.7 12.7 %collective-permute-start.3 = (f32[48,4,128]{2,1,0:T(4,128)S(1)}, f32[48,4,128]{2,1,0:T(4,128)S(1)}, u32[]{:S(2)}, u32[]{:S(2)}) collective-permute-start(f32[48,4,128]{2,1,0:T(4,128)S(1)} %copy-done.2), channel_id=1, source_target_pairs={{0,1},{1,2},{2,3},{3,0},{4,5},{5,6},{6,7},{7,4},{8,9},{9,10},{10,1... | collective-permute-start | bytes 294920 | tf_op jit(solution)/shard_map/ppermute | solution.py:418
  64.0 10.0 %collective-permute-start.5 = (f32[48,4,128]{2,1,0:T(4,128)S(1)}, f32[48,4,128]{2,1,0:T(4,128)S(1)}, u32[]{:S(2)}, u32[]{:S(2)}) collective-permute-start(f32[48,4,128]{2,1,0:T(4,128)S(1)} %collective-permute-done.4.refs_7_), channel_id=1, source_target_pairs={{0,3},{1,0},{2,1},{3,2},{4,7},{5,4},{6,5},{7,6},{8,11},{9,8},{10,9... | collective-permute-start | bytes 294920 | tf_op jit(solution)/shard_map/ppermute | solution.py:418
where the time goes:
time: 79.4 us; the launch traced here: 78.8 us
  Pallas kernels  30.1 us (38%)
  starting transfers between devices  24.5 us (31%)
  waiting for transfers between devices  19.8 us (25%)
  local copies, waits for them, and re-layouts  2.85 us (4%)
  between operations  1.43 us (2%)
    ppermute x6, waiting for transfers between devices, shift(): lax.ppermute(array, 'xg', [(i, (i + by) % groups) for i in range(groups)])  17.2 us
    ppermute x6, starting transfers between devices, shift(): lax.ppermute(array, 'xg', [(i, (i + by) % groups) for i in range(groups)])  14.6 us
    all_to_all x2, starting transfers between devices, exchange(): lax.all_to_all(array, ('atm', 'xg'), split_axis=0, concat_axis=0, tiled=T...  9.96 us
    pallas_call x1, Pallas kernels, margins_stage(): pl.pallas_call(functools.partial(margin_kernel, groups, rows, slots, gain...  9.58 us
    pallas_call x2, Pallas kernels, split_weights(): pl.pallas_call(split_kernel, grid=(count // step,), out_shape=jax.ShapeDt...  9.47 us
    pallas_call x1, Pallas kernels, finish(): pl.pallas_call(functools.partial(finish_kernel, groups, blocks // groups,...  4.85 us
    pallas_call x1, Pallas kernels, bottoms(): pl.pallas_call(functools.partial(bottom_kernel, groups, own, rows, slots)...  4.18 us
    all_to_all x2, waiting for transfers between devices, exchange(): lax.all_to_all(array, ('atm', 'xg'), split_axis=0, concat_axis=0, tiled=T...  2.6 us
  transfers between devices with their start and end apart: 8, of which 6 were waited for; matrix products, arithmetic and copies ran while one was open for 2% of the time, Pallas kernels for 12%

commit v1 on v0

--- a/solution.py
+++ b/solution.py
@@ -37,8 +37,10 @@
 
 
 def split(value):
+    tall, width = value.shape
     high = value.astype(BF16).astype(F32)
-    return jnp.concatenate([high, value - high], 0).astype(BF16)
+    gap = jnp.zeros((round_up(tall, 2 * ROWS) - tall, width), F32)
+    return jnp.concatenate([high, gap, value - high, gap], 0).astype(BF16)
 
 
 def factor_kernel(levels, own, upper_hbm, lower_hbm, gain_hbm, first_ref, second_ref,
@@ -259,7 +261,7 @@
                     value_ref[slot_ref[k], :top], weight_ref[k, columns:], (((1,), (1,)), ((), ())),
                     preferred_element_type=F32,
                 )
-                cell_ref[target] += one[:tall] + (one[tall:] + two[:tall])
+                cell_ref[target] += one[:tall] + (one[top:top + tall] + two[:tall])
 
     for j in range(cells):
         cell = cell_ref[j]
@@ -279,7 +281,7 @@
             two = jnp.dot(
                 two_ref[block_ref[k], :top], weight_ref[k, columns:], preferred_element_type=F32
             )
-            back_ref[target] += one[:tall] + (one[tall:] + two[:tall])
+            back_ref[target] += one[:tall] + (one[top:top + tall] + two[:tall])
 
     for a in range(sources):
         for p in range(slots):
@@ -309,9 +311,9 @@
         out_specs=(vmem(), vmem()),
         scratch_shapes=[
             pltpu.VMEM((margins, twice, columns), BF16),
-            pltpu.VMEM((sources * slots, 2 * tall, width), BF16),
+            pltpu.VMEM((sources * slots, 2 * round_up(tall, 2 * ROWS), width), BF16),
             pltpu.VMEM((cells + 1, tall, width), F32),
-            pltpu.VMEM((cells, 2 * tall, width), BF16),
+            pltpu.VMEM((cells, 2 * round_up(tall, 2 * ROWS), width), BF16),
             pltpu.VMEM((sources * slots + 1, tall, width), F32),
             pltpu.VMEM((sources * slots, tall, width), F32),
             pltpu.SemaphoreType.DMA((chunks,)),

time: 79.4 us -> 79.5 us (level)
  no operation moved by 1% of the time
where the time goes in v1:
time: 79.5 us; the launch traced here: 78.9 us
  Pallas kernels  30.2 us (38%)
  starting transfers between devices  24.6 us (31%)
  waiting for transfers between devices  19.8 us (25%)
  local copies, waits for them, and re-layouts  2.85 us (4%)
  between operations  1.43 us (2%)
    ppermute x6, waiting for transfers between devices, shift(): lax.ppermute(array, 'xg', [(i, (i + by) % groups) for i in range(groups)])  17.2 us
    ppermute x6, starting transfers between devices, shift(): lax.ppermute(array, 'xg', [(i, (i + by) % groups) for i in range(groups)])  14.6 us
    all_to_all x2, starting transfers between devices, exchange(): lax.all_to_all(array, ('atm', 'xg'), split_axis=0, concat_axis=0, tiled=T...  10 us
    pallas_call x1, Pallas kernels, margins_stage(): pl.pallas_call(functools.partial(margin_kernel, groups, rows, slots, gain...  9.59 us
    pallas_call x2, Pallas kernels, split_weights(): pl.pallas_call(split_kernel, grid=(count // step,), out_shape=jax.ShapeDt...  9.47 us
    pallas_call x1, Pallas kernels, finish(): pl.pallas_call(functools.partial(finish_kernel, groups, blocks // groups,...  4.85 us
    pallas_call x1, Pallas kernels, bottoms(): pl.pallas_call(functools.partial(bottom_kernel, groups, own, rows, slots)...  4.18 us
    all_to_all x2, waiting for transfers between devices, exchange(): lax.all_to_all(array, ('atm', 'xg'), split_axis=0, concat_axis=0, tiled=T...  2.6 us
  transfers between devices with their start and end apart: 8, of which 6 were waited for; matrix products, arithmetic and copies ran while one was open for 2% of the time, Pallas kernels for 12%

profile of v1, /device:TPU:0, one launch (start us, length us, event | category | flops | bytes accessed | tf_op | source)
XLA Modules:
  0.0 78.9 jit_solution(6514608316860566518)
XLA Ops:
  0.6 2.1 %factors.1 = (f32[49,4,128]{2,1,0:T(4,128)}, f32[48,4,128]{2,1,0:T(4,128)}) custom-call(f32[192,128]{1,0:T(8,128)} %bitcast.29, f32[192,128]{1,0:T(8,128)} %bitcast.30, f32[4,128]{1,0:T(4,128)} %gain_hbm.1), custom_call_target="tpu_custom_call" | custom-call | flops 1000000 | bytes 400000 | tf_op jit(solution)/shard_map/factors/pallas_call | solution.py:74
  2.7 3.1 %collective-permute-start = (f32[49,4,128]{2,1,0:T(4,128)}, f32[49,4,128]{2,1,0:T(4,128)S(1)}, u32[]{:S(2)}, u32[]{:S(2)}) collective-permute-start(f32[49,4,128]{2,1,0:T(4,128)} %get-tuple-element.6.refs_0_), channel_id=1, source_target_pairs={{0,1},{1,2},{2,3},{3,0},{4,5},{5,6},{6,7},{7,4},{8,9},{9,10},{10,1... | collective-permute-start | bytes 301064 | tf_op jit(solution)/shard_map/ppermute | solution.py:420
  5.8 2.6 %collective-permute-start.1 = (f32[49,4,128]{2,1,0:T(4,128)}, f32[49,4,128]{2,1,0:T(4,128)S(1)}, u32[]{:S(2)}, u32[]{:S(2)}) collective-permute-start(f32[49,4,128]{2,1,0:T(4,128)} %get-tuple-element.6.refs_0_), channel_id=1, source_target_pairs={{0,2},{1,3},{2,0},{3,1},{4,6},{5,7},{6,4},{7,5},{8,10},{9,11},{10,... | collective-permute-start | bytes 301064 | tf_op jit(solution)/shard_map/ppermute | solution.py:420
  8.4 1.3 %collective-permute-start.2 = (f32[49,4,128]{2,1,0:T(4,128)}, f32[49,4,128]{2,1,0:T(4,128)S(1)}, u32[]{:S(2)}, u32[]{:S(2)}) collective-permute-start(f32[49,4,128]{2,1,0:T(4,128)} %get-tuple-element.6.refs_0_), channel_id=1, source_target_pairs={{0,3},{1,0},{2,1},{3,2},{4,7},{5,4},{6,5},{7,6},{8,11},{9,8},{10,9... | collective-permute-start | bytes 301064 | tf_op jit(solution)/shard_map/ppermute | solution.py:420
  9.8 0.8 copy.18
  10.5 0.1 reshape_squeeze.3
  10.6 1.1 %collective-permute-done.refs_1_ = f32[49,4,128]{2,1,0:T(4,128)S(1)} collective-permute-done((f32[49,4,128]{2,1,0:T(4,128)}, f32[49,4,128]{2,1,0:T(4,128)S(1)}, u32[]{:S(2)}, u32[]{:S(2)}) %collective-permute-start) | collective-permute-done | bytes 100384 | tf_op jit(solution)/shard_map/ppermute | solution.py:420
  11.8 3.5 %collective-permute-done.1.refs_2_ = f32[49,4,128]{2,1,0:T(4,128)S(1)} collective-permute-done((f32[49,4,128]{2,1,0:T(4,128)}, f32[49,4,128]{2,1,0:T(4,128)S(1)}, u32[]{:S(2)}, u32[]{:S(2)}) %collective-permute-start.1) | collective-permute-done | bytes 100384 | tf_op jit(solution)/shard_map/ppermute | solution.py:420
  15.3 0.0 collective-permute-done.2.refs_3_
  15.3 0.0 copy-start
  15.3 0.9 %copy-done = f32[49,4,128]{2,1,0:T(4,128)S(1)} copy-done((f32[49,4,128]{2,1,0:T(4,128)S(1)}, f32[49,4,128]{2,1,0:T(4,128)}, u32[]{:S(2)}) %copy-start) | copy-done | bytes 100376
  16.2 0.0 copy-start.8
  16.2 4.2 %bottoms.1 = f32[896,128]{1,0:T(8,128)} custom-call(s32[1]{0:T(128)} %bitcast.me_ref, s32[64]{0:T(128)S(1)} %compare_select_fusion.2.place_ref, f32[49,4,128]{2,1,0:T(4,128)S(1)} %copy-done, f32[49,4,128]{2,1,0:T(4,128)S(1)} %collective-permute-done.refs_1_, f32[49,4,128]{2,1,0:T(4,128)S(1)} %collective-permute-done.1.refs_2_, ...), custom_call_target="tpu_custom_call" | custom-call | flops 4000000 | bytes 7000000 | tf_op jit(solution)/shard_map/bottoms/pallas_call | solution.py:168
  20.4 5.9 %all-to-all-start = ((f32[32,14,2,128]{3,2,1,0:T(2,128)}), f32[32,14,2,128]{3,2,1,0:T(2,128)S(1)}, u32[]{:S(2)}, u32[]{:S(2)}) async-start(f32[32,14,2,128]{3,2,1,0:T(2,128)} %bitcast.7), calls=%async_computation | async-start | bytes 917504 | tf_op jit(solution)/shard_map/all_to_all | solution.py:427
  26.3 0.0 copy-done.8
  26.4 0.2 copy.19.surface_ref
  27.2 8.1 %split_weights.3.weight_b = bf16[80,256,128]{2,1,0:T(8,128)(2,1)} custom-call(f32[96,128,128]{2,1,0:T(8,128)} %bitcast.20), custom_call_target="tpu_custom_call" | custom-call | flops 2500000 | bytes 6500000 | tf_op jit(solution)/shard_map/split_weights/pallas_call | solution.py:200
  35.3 0.0 copy-start.3
  35.3 0.0 copy-start.4
  35.3 0.0 copy-start.5
  35.3 0.0 copy-start.6
  35.3 0.0 copy-start.7
  35.3 1.3 %split_weights.2.weight_a = bf16[16,256,128]{2,1,0:T(8,128)(2,1)S(1)} custom-call(f32[96,128,128]{2,1,0:T(8,128)} %bitcast.21), custom_call_target="tpu_custom_call" | custom-call | flops 2500000 | bytes 6500000 | tf_op jit(solution)/shard_map/split_weights/pallas_call | solution.py:200
  36.7 0.0 copy-start.2
  36.7 0.0 copy-start.1
  36.7 2.6 %all-to-all-done = f32[32,14,2,128]{3,2,1,0:T(2,128)S(1)} async-done(((f32[32,14,2,128]{3,2,1,0:T(2,128)}), f32[32,14,2,128]{3,2,1,0:T(2,128)S(1)}, u32[]{:S(2)}, u32[]{:S(2)}) %all-to-all-start) | async-done | bytes 458784 | tf_op jit(solution)/shard_map/all_to_all | solution.py:427
  39.3 0.0 copy-done.3
  39.3 0.0 copy-done.4
  39.3 0.0 copy-done.5
  39.3 0.0 copy-done.6
  39.3 0.0 copy-done.7
  39.3 9.6 %margins.1 = (f32[896,128]{1,0:T(8,128)}, f32[16,56,128]{2,1,0:T(8,128)S(1)}) custom-call(s32[96]{0:T(128)S(1)} %bitcast.18, s32[96]{0:T(128)S(1)} %bitcast.19, s32[1]{0:T(128)S(6)} %copy.21.count_ref, bf16[16,256,128]{2,1,0:T(8,128)(2,1)S(1)} %split_weights.2.weight_a, bf16[80,256,128]{2,1,0:T(8,128)(2,1)} %split_weights.3.weight_b, ...), custom_call_target="tpu_custom_call" | custom-call | flops 800000000 | bytes 8000000 | tf_op jit(solution)/shard_map/margins/pallas_call | solution.py:304
  48.9 4.1 %all-to-all-start.1 = ((f32[32,14,2,128]{3,2,1,0:T(2,128)}), f32[32,14,2,128]{3,2,1,0:T(2,128)S(1)}, u32[]{:S(2)}, u32[]{:S(2)}) async-start(f32[32,14,2,128]{3,2,1,0:T(2,128)} %bitcast.11), calls=%async_computation.1 | async-start | bytes 917504 | tf_op jit(solution)/shard_map/all_to_all | solution.py:427
  53.1 0.0 copy-done.2
  53.1 3.7 %collective-permute-start.4 = (f32[48,4,128]{2,1,0:T(4,128)S(1)}, f32[48,4,128]{2,1,0:T(4,128)S(1)}, u32[]{:S(2)}, u32[]{:S(2)}) collective-permute-start(f32[48,4,128]{2,1,0:T(4,128)S(1)} %copy-done.2), channel_id=1, source_target_pairs={{0,3},{1,0},{2,1},{3,2},{4,7},{5,4},{6,5},{7,6},{8,11},{9,8},{10,9... | collective-permute-start | bytes 294920 | tf_op jit(solution)/shard_map/ppermute | solution.py:420
  56.7 0.0 collective-permute-start.3
  56.7 7.3 %collective-permute-done.4.refs_7_ = f32[48,4,128]{2,1,0:T(4,128)S(1)} collective-permute-done((f32[48,4,128]{2,1,0:T(4,128)S(1)}, f32[48,4,128]{2,1,0:T(4,128)S(1)}, u32[]{:S(2)}, u32[]{:S(2)}) %collective-permute-start.4) | collective-permute-done | bytes 98336 | tf_op jit(solution)/shard_map/ppermute | solution.py:420
  64.0 3.8 %collective-permute-start.5 = (f32[48,4,128]{2,1,0:T(4,128)S(1)}, f32[48,4,128]{2,1,0:T(4,128)S(1)}, u32[]{:S(2)}, u32[]{:S(2)}) collective-permute-start(f32[48,4,128]{2,1,0:T(4,128)S(1)} %collective-permute-done.4.refs_7_), channel_id=1, source_target_pairs={{0,3},{1,0},{2,1},{3,2},{4,7},{5,4},{6,5},{7,6},{8,11},{9,8},{10,9... | collective-permute-start | bytes 294920 | tf_op jit(solution)/shard_map/ppermute | solution.py:420
  67.9 0.1 copy.20
  68.0 0.8 %slice.4 = f32[16,4,13,128]{3,0,2,1:T(8,128)} slice(f32[16,4,14,128]{3,0,2,1:T(8,128)S(1)} %bitcast.26), slice={[0:16], [0:4], [0:13], [0:128]} | slice | bytes 851968 | tf_op jit(solution)/shard_map/slice | solution.py:457
  68.8 0.7 collective-permute-done.3.refs_5_
  69.4 4.6 %collective-permute-done.5.refs_6_ = f32[48,4,128]{2,1,0:T(4,128)S(1)} collective-permute-done((f32[48,4,128]{2,1,0:T(4,128)S(1)}, f32[48,4,128]{2,1,0:T(4,128)S(1)}, u32[]{:S(2)}, u32[]{:S(2)}) %collective-permute-start.5) | collective-permute-done | bytes 98336 | tf_op jit(solution)/shard_map/ppermute | solution.py:420
  74.0 0.0 all-to-all-done.1
  74.0 0.0 copy-done.1
  74.0 4.9 %finish.1 = f32[16,13,48,128]{3,2,1,0:T(8,128)} custom-call(s32[1]{0:T(128)} %bitcast.me_ref, s32[64]{0:T(128)S(1)} %compare_select_fusion.2.place_ref, f32[896,128]{1,0:T(8,128)S(1)} %bitcast.17, f32[49,4,128]{2,1,0:T(4,128)S(1)} %copy-done.1, f32[49,4,128]{2,1,0:T(4,128)S(1)} %collective-permute-done.refs_1_, ...), custom_call_target="tpu_custom_call" | custom-call | flops 8000000 | bytes 12000000 | tf_op jit(solution)/shard_map/finish/pallas_call | solution.py:388
  (2 shorter events, 0.1 us)
Async XLA Ops:
  2.7 9.1 %collective-permute-start = (f32[49,4,128]{2,1,0:T(4,128)}, f32[49,4,128]{2,1,0:T(4,128)S(1)}, u32[]{:S(2)}, u32[]{:S(2)}) collective-permute-start(f32[49,4,128]{2,1,0:T(4,128)} %get-tuple-element.6.refs_0_), channel_id=1, source_target_pairs={{0,1},{1,2},{2,3},{3,0},{4,5},{5,6},{6,7},{7,4},{8,9},{9,10},{10,1... | collective-permute-start | bytes 301064 | tf_op jit(solution)/shard_map/ppermute | solution.py:420
  5.8 9.5 %collective-permute-start.1 = (f32[49,4,128]{2,1,0:T(4,128)}, f32[49,4,128]{2,1,0:T(4,128)S(1)}, u32[]{:S(2)}, u32[]{:S(2)}) collective-permute-start(f32[49,4,128]{2,1,0:T(4,128)} %get-tuple-element.6.refs_0_), channel_id=1, source_target_pairs={{0,2},{1,3},{2,0},{3,1},{4,6},{5,7},{6,4},{7,5},{8,10},{9,11},{10,... | collective-permute-start | bytes 301064 | tf_op jit(solution)/shard_map/ppermute | solution.py:420
  8.4 6.9 %collective-permute-start.2 = (f32[49,4,128]{2,1,0:T(4,128)}, f32[49,4,128]{2,1,0:T(4,128)S(1)}, u32[]{:S(2)}, u32[]{:S(2)}) collective-permute-start(f32[49,4,128]{2,1,0:T(4,128)} %get-tuple-element.6.refs_0_), channel_id=1, source_target_pairs={{0,3},{1,0},{2,1},{3,2},{4,7},{5,4},{6,5},{7,6},{8,11},{9,8},{10,9... | collective-permute-start | bytes 301064 | tf_op jit(solution)/shard_map/ppermute | solution.py:420
  15.3 0.9 %copy-start = (f32[49,4,128]{2,1,0:T(4,128)S(1)}, f32[49,4,128]{2,1,0:T(4,128)}, u32[]{:S(2)}) copy-start(f32[49,4,128]{2,1,0:T(4,128)} %get-tuple-element.6.refs_0_) | copy-start | bytes 301060
  16.2 10.1 %copy-start.8 = (f32[16,52,128]{2,0,1:T(8,128)S(1)}, f32[16,52,128]{2,0,1:T(8,128)}, u32[]{:S(2)}) copy-start(f32[16,52,128]{2,0,1:T(8,128)} %param.22) | copy-start | bytes 1277956
  20.4 18.9 %all-to-all-start = ((f32[32,14,2,128]{3,2,1,0:T(2,128)}), f32[32,14,2,128]{3,2,1,0:T(2,128)S(1)}, u32[]{:S(2)}, u32[]{:S(2)}) async-start(f32[32,14,2,128]{3,2,1,0:T(2,128)} %bitcast.7), calls=%async_computation | async-start | bytes 917504 | tf_op jit(solution)/shard_map/all_to_all | solution.py:427
  35.3 4.0 %copy-start.3 = (f32[16,128]{1,0:T(8,128)S(1)}, f32[16,128]{1,0:T(8,128)}, u32[]{:S(2)}) copy-start(f32[16,128]{1,0:T(8,128)} %coef_ref.1) | copy-start | bytes 24580
  35.3 4.0 %copy-start.4 = (s32[16,128]{1,0:T(8,128)S(1)}, s32[16,128]{1,0:T(8,128)}, u32[]{:S(2)}) copy-start(s32[16,128]{1,0:T(8,128)} %mask_ref.1) | copy-start | bytes 24580
  35.3 4.0 %copy-start.5 = (f32[16,128]{1,0:T(8,128)S(1)}, f32[16,128]{1,0:T(8,128)}, u32[]{:S(2)}) copy-start(f32[16,128]{1,0:T(8,128)} %land_ref.1) | copy-start | bytes 24580
  35.3 4.0 %copy-start.6 = (s32[1,96]{1,0:T(1,128)S(1)}, s32[1,96]{1,0:T(1,128)}, u32[]{:S(2)}) copy-start(s32[1,96]{1,0:T(1,128)} %param.18) | copy-start | bytes 1156
  35.3 4.0 %copy-start.7 = (s32[1,96]{1,0:T(1,128)S(1)}, s32[1,96]{1,0:T(1,128)}, u32[]{:S(2)}) copy-start(s32[1,96]{1,0:T(1,128)} %param.19) | copy-start | bytes 1156
  36.7 16.4 %copy-start.2 = (f32[48,4,128]{2,1,0:T(4,128)S(1)}, f32[48,4,128]{2,1,0:T(4,128)}, u32[]{:S(2)}) copy-start(f32[48,4,128]{2,1,0:T(4,128)} %get-tuple-element.8.refs_4_) | copy-start | bytes 294916
  36.7 37.3 %copy-start.1 = (f32[49,4,128]{2,1,0:T(4,128)S(1)}, f32[49,4,128]{2,1,0:T(4,128)}, u32[]{:S(2)}) copy-start(f32[49,4,128]{2,1,0:T(4,128)} %get-tuple-element.6.refs_0_) | copy-start | bytes 301060
  48.9 25.1 %all-to-all-start.1 = ((f32[32,14,2,128]{3,2,1,0:T(2,128)}), f32[32,14,2,128]{3,2,1,0:T(2,128)S(1)}, u32[]{:S(2)}, u32[]{:S(2)}) async-start(f32[32,14,2,128]{3,2,1,0:T(2,128)} %bitcast.11), calls=%async_computation.1 | async-start | bytes 917504 | tf_op jit(solution)/shard_map/all_to_all | solution.py:427
  53.1 11.0 %collective-permute-start.4 = (f32[48,4,128]{2,1,0:T(4,128)S(1)}, f32[48,4,128]{2,1,0:T(4,128)S(1)}, u32[]{:S(2)}, u32[]{:S(2)}) collective-permute-start(f32[48,4,128]{2,1,0:T(4,128)S(1)} %copy-done.2), channel_id=1, source_target_pairs={{0,3},{1,0},{2,1},{3,2},{4,7},{5,4},{6,5},{7,6},{8,11},{9,8},{10,9... | collective-permute-start | bytes 294920 | tf_op jit(solution)/shard_map/ppermute | solution.py:420
  56.7 12.7 %collective-permute-start.3 = (f32[48,4,128]{2,1,0:T(4,128)S(1)}, f32[48,4,128]{2,1,0:T(4,128)S(1)}, u32[]{:S(2)}, u32[]{:S(2)}) collective-permute-start(f32[48,4,128]{2,1,0:T(4,128)S(1)} %copy-done.2), channel_id=1, source_target_pairs={{0,1},{1,2},{2,3},{3,0},{4,5},{5,6},{6,7},{7,4},{8,9},{9,10},{10,1... | collective-permute-start | bytes 294920 | tf_op jit(solution)/shard_map/ppermute | solution.py:420
  64.0 10.0 %collective-permute-start.5 = (f32[48,4,128]{2,1,0:T(4,128)S(1)}, f32[48,4,128]{2,1,0:T(4,128)S(1)}, u32[]{:S(2)}, u32[]{:S(2)}) collective-permute-start(f32[48,4,128]{2,1,0:T(4,128)S(1)} %collective-permute-done.4.refs_7_), channel_id=1, source_target_pairs={{0,3},{1,0},{2,1},{3,2},{4,7},{5,4},{6,5},{7,6},{8,11},{9,8},{10,9... | collective-permute-start | bytes 294920 | tf_op jit(solution)/shard_map/ppermute | solution.py:420
